TPU v7x, 128 devices: a whole 4x4x4 slice. The times are simulated.
128 devices in a mesh: req: 32 (over z, y, core), head: 4 (over x).
Axes of the slice: x: 4, y: 4, z: 4, core: 2. Of those that a mesh axis runs over, the one named last changes fastest.
Arguments:
- tokens: bfloat16 [128, 64, 2048], P(('req', 'head')), may hold values from -3 to 3
- live: int32 [128, 64], P(('req', 'head')), may hold values from 0 to 1, as said below
- parents: int32 [128, 64], P('req'), may hold values from -1 to 62, as said below
- lengths: int32 [128], P('req'), may hold values from 1 to 2048, as said below
- accepted: int32 [128, 8], P('req'), may hold values from 0 to 31, as said below
- routes: int32 [128, 64, 6], P(('req', 'head')), may hold values from 0 to 63, all different within a row; in each aligned block of 64 rows (0 to 63, 64 to 127, ..., all dimensions but the last counted through in order) at most 8 rows name the same one
- cache: bfloat16 [128, 4, 2048, 256], P('req', 'head'), may hold values from -160 to 160, as said below
- attn_gain: float32 [2048], replicated, may hold values from 0.1 to 1.9
- w_qkv: bfloat16 [2048, 3072], P(None, 'head'), may hold values from -0.125 to 0.125
- w_out: bfloat16 [2048, 2048], P('head'), may hold values from -0.125 to 0.125
- ffn_gain: float32 [2048], replicated, may hold values from 0.1 to 1.9
- shared_gate: bfloat16 [2048, 1408], P(None, 'head'), may hold values from -0.125 to 0.125
- shared_up: bfloat16 [2048, 1408], P(None, 'head'), may hold values from -0.125 to 0.125
- shared_down: bfloat16 [1408, 2048], P('head'), may hold values from -0.15625 to 0.15625
- router: bfloat16 [2048, 64], replicated, may hold values from -0.125 to 0.125
- expert_in: bfloat16 [128, 2048, 1408], P(('req', 'head')), may hold values from -0.125 to 0.125
- expert_out: bfloat16 [128, 704, 2048], P(('req', 'head')), may hold values from -0.21875 to 0.21875
Outputs:
- hidden_out: bfloat16 [128, 64, 2048], P(('req', 'head'))
- accepted_kv: bfloat16 [128, 4, 8, 256], P('req', 'head')
Inputs may be any that keep to these rules, and one draw needn't show every extreme that they name: lengths run from 1 to 2048; every draw has a request with all 2048 slots filled. Each request's live entries are its first ones; at least 32 are live and some request has all 64 live. parents[r, 0] = -1 and parents[r, i] < i for i > 0. `accepted`: each request's entries are distinct, ascending, begin with 0 and name live nodes; some request names node 31. `routes`: within the 64 nodes of one request no expert is named more than 8 times, and in some request one expert is named exactly 8 times; the 6 experts of a node differ. `cache`: entries are finite.
All inputs are finite; a program needn't handle non-finite values.
Results may differ from a plain program's by a relative error of at most 0.012.
The roundings to bfloat16 on the way count: a program that leaves them out, or rounds other values in their place, can miss the bound.
Values may be sent and summed in bfloat16 or wider, within the bound.
A program may use at most 128 MiB of HBM per device.

v0:
```python
import math

import jax
import jax.numpy as jnp
from jax import lax
from jax.sharding import PartitionSpec as P

EPSILON = 1e-06
ROPE_BASE = 10000.0


def rms_norm(values, gain):
    wide = values.astype(jnp.float32)
    power = jnp.mean(wide * wide, axis=-1, keepdims=True)
    return (wide * lax.rsqrt(power + EPSILON) * gain).astype(jnp.bfloat16)


def rotate(values, position):
    half = values.shape[-1] // 2
    frequency = ROPE_BASE ** (-jnp.arange(half, dtype=jnp.float32) / half)
    angle = position[..., None] * frequency
    cosine = jnp.cos(angle)
    sine = jnp.sin(angle)
    first = values[..., :half]
    second = values[..., half:]
    return jnp.concatenate(
        [first * cosine - second * sine, second * cosine + first * sine], axis=-1
    )


def ancestry(parents):
    nodes_count = parents.shape[-1]
    nodes = jnp.arange(nodes_count, dtype=jnp.int32)
    reach = (parents[..., :, None] == nodes).astype(jnp.float32) + jnp.eye(
        nodes_count, dtype=jnp.float32
    )
    for turn in range(nodes_count.bit_length()):
        reach = jnp.minimum(
            jnp.einsum("rij,rjk->rik", reach, reach, precision=lax.Precision.HIGHEST), 1.0
        )
    depth = jnp.sum(reach, axis=-1) - 1.0
    return (reach, depth)


def head_group(projected, position, length, reach, cache_rows):
    group = projected.shape[0] - 2
    tree = projected.shape[1]
    head_dim = projected.shape[2]
    query = rotate(projected[:group], position).astype(jnp.bfloat16).reshape(group * tree, head_dim)
    key_new = rotate(projected[group], position).astype(jnp.bfloat16)
    value_new = projected[group + 1].astype(jnp.bfloat16)
    scale = 1.0 / math.sqrt(head_dim)
    cache_keys = cache_rows[:, :head_dim]
    cache_values = cache_rows[:, head_dim:]
    old_scores = (
        jnp.einsum("qd,kd->qk", query, cache_keys, preferred_element_type=jnp.float32) * scale
    )
    new_scores = jnp.einsum("qd,kd->qk", query, key_new, preferred_element_type=jnp.float32) * scale
    visible = jnp.arange(cache_rows.shape[0], dtype=jnp.int32) < length
    old_scores = jnp.where(visible[None, :], old_scores, -1e30)
    new_scores = jnp.where(jnp.tile(reach, (group, 1)) > 0.5, new_scores, -1e30)
    peak = jnp.maximum(
        jnp.max(old_scores, axis=-1, keepdims=True), jnp.max(new_scores, axis=-1, keepdims=True)
    )
    old_weights = jnp.exp(old_scores - peak)
    new_weights = jnp.exp(new_scores - peak)
    denominator = jnp.sum(old_weights, axis=-1, keepdims=True) + jnp.sum(
        new_weights, axis=-1, keepdims=True
    )
    old_probs = (old_weights / denominator).astype(jnp.bfloat16)
    new_probs = (new_weights / denominator).astype(jnp.bfloat16)
    mixed = jnp.dot(old_probs, cache_values, preferred_element_type=jnp.float32) + jnp.dot(
        new_probs, value_new, preferred_element_type=jnp.float32
    )
    mixed = (
        mixed.astype(jnp.bfloat16)
        .reshape(group, tree, head_dim)
        .transpose(1, 0, 2)
        .reshape(tree, group * head_dim)
    )
    return (mixed, jnp.concatenate([key_new, value_new], axis=-1))


def expert_half(rows, inner, outer):
    both = jnp.dot(rows, inner, preferred_element_type=jnp.float32)
    half = inner.shape[1] // 2
    hidden = (jax.nn.silu(both[:, :half]) * both[:, half:]).astype(jnp.bfloat16)
    return jnp.dot(hidden, outer, preferred_element_type=jnp.float32).astype(jnp.bfloat16)


def body(
    tokens,
    live,
    parents,
    lengths,
    accepted,
    routes,
    cache,
    attn_gain,
    w_qkv,
    w_out,
    ffn_gain,
    shared_gate,
    shared_up,
    shared_down,
    router,
    expert_in,
    expert_out,
):
    tree = tokens.shape[1]
    width = tokens.shape[2]
    own_rows = tokens[0]
    group_count = lax.axis_size("head")
    head_index = lax.axis_index("head")
    local_heads = cache.shape[1]
    head_dim = cache.shape[3] // 2
    group = w_qkv.shape[1] // (local_heads * head_dim) - 2
    projected = jnp.dot(
        rms_norm(lax.all_gather(own_rows, "head", axis=0, tiled=True), attn_gain),
        w_qkv,
        preferred_element_type=jnp.float32,
    )
    projected = projected.reshape(group_count, tree, local_heads, group + 2, head_dim).transpose(
        0, 2, 3, 1, 4
    )
    reach, depth = ancestry(parents)
    positions = lengths[:, None].astype(jnp.float32) + depth
    inner_map = jax.vmap(head_group, in_axes=(0, None, None, None, 0))
    mixed, fresh = jax.vmap(inner_map)(projected, positions, lengths, reach, cache)
    mixed = mixed.transpose(0, 2, 1, 3).reshape(group_count * tree, local_heads * group * head_dim)
    accepted_kv = jnp.take_along_axis(fresh, accepted[:, None, :, None], axis=2)
    own_start = head_index * tree
    term = jnp.dot(mixed, w_out, preferred_element_type=jnp.float32)
    own_term = lax.dynamic_slice_in_dim(term, own_start, tree, 0) + own_rows.astype(jnp.float32)
    term = lax.dynamic_update_slice_in_dim(term, own_term, own_start, 0)
    resid_all = lax.psum(term, "head").astype(jnp.bfloat16)
    normed_all = rms_norm(resid_all, ffn_gain)
    resid = lax.dynamic_slice_in_dim(resid_all, own_start, tree, 0)
    normed = lax.dynamic_slice_in_dim(normed_all, own_start, tree, 0)
    gated = jax.nn.silu(jnp.dot(normed_all, shared_gate, preferred_element_type=jnp.float32))
    hidden = (gated * jnp.dot(normed_all, shared_up, preferred_element_type=jnp.float32)).astype(
        jnp.bfloat16
    )
    shared = lax.psum_scatter(
        jnp.dot(hidden, shared_down, preferred_element_type=jnp.float32).astype(jnp.bfloat16),
        "head",
        scatter_dimension=0,
        tiled=True,
    ).astype(jnp.float32)
    choose = routes[0]
    top_count = choose.shape[1]
    expert_count = router.shape[1]
    capacity = 4 * tree * top_count // (3 * expert_count)
    logits = jnp.dot(normed, router, preferred_element_type=jnp.float32)
    picked = jax.nn.sigmoid(jnp.take_along_axis(logits, choose, axis=1))
    gates = picked / jnp.sum(picked, axis=-1, keepdims=True)
    route_flat = choose.reshape(-1)
    onehot = (route_flat[:, None] == jnp.arange(expert_count, dtype=jnp.int32)).astype(jnp.int32)
    slots = jnp.sum((jnp.cumsum(onehot, axis=0) - onehot) * onehot, axis=-1)
    target = (route_flat * capacity + slots).reshape(tree, top_count)
    placing = jnp.any(
        target[:, :, None] == jnp.arange(expert_count * capacity, dtype=jnp.int32), axis=1
    ).astype(jnp.bfloat16)
    outgoing = jnp.einsum("ts,td->sd", placing, normed, preferred_element_type=jnp.float32).astype(
        jnp.bfloat16
    )
    outgoing = jnp.repeat(outgoing.reshape(expert_count, capacity, width), 2, axis=0)
    inner = expert_in[0]
    outer = expert_out[0]
    received = lax.all_to_all(outgoing, ("req", "head"), split_axis=0, concat_axis=0, tiled=True)
    partial_value = expert_half(received.reshape(-1, width), inner, outer).reshape(received.shape)
    returned = lax.all_to_all(
        partial_value, ("req", "head"), split_axis=0, concat_axis=0, tiled=True
    )
    halves = returned.reshape(expert_count, 2, capacity, width).astype(jnp.float32)
    expert_rows = (halves[:, 0] + halves[:, 1]).reshape(expert_count * capacity, width)
    routed = jnp.sum(gates[:, :, None] * expert_rows[target], axis=1)
    total_out = resid.astype(jnp.float32) + shared + routed
    hidden_out = jnp.where(live[0][:, None] == 1, total_out, 0.0).astype(jnp.bfloat16)
    return (hidden_out[None], accepted_kv)


def solution(mesh):
    in_specs = (
        P(("req", "head"), None, None),
        P(("req", "head"), None),
        P("req", None),
        P("req"),
        P("req", None),
        P(("req", "head"), None, None),
        P("req", "head", None, None),
        P(),
        P(None, "head"),
        P("head", None),
        P(),
        P(None, "head"),
        P(None, "head"),
        P("head", None),
        P(),
        P(("req", "head"), None, None),
        P(("req", "head"), None, None),
    )
    out_specs = (P(("req", "head"), None, None), P("req", "head", None, None))
    return jax.shard_map(body, mesh=mesh, in_specs=in_specs, out_specs=out_specs, check_vma=False)
```

profile of v0, /device:TPU:1, one launch (start us, length us, event | category | flops | bytes accessed | tf_op | source)
XLA Modules:
  0.0 269.0 jit_solution(10102755729981100320)
XLA Ops:
  7.9 0.9 copy.72
  9.8 0.9 reduce-window.6
  11.3 1.1 convolution_minimum_fusion.6
  14.4 0.9 gt.12
  15.4 0.8 fusion.28
  16.8 0.7 iota_compare_fusion.6
  17.5 17.4 %all-gather.3.cloned.1.call-done = bf16[1,256,2048]{2,1,0:T(8,128)(2,1)} async-done(((bf16[1,64,2048]{2,1,0:T(8,128)(2,1)}), bf16[1,256,2048]{2,1,0:T(8,128)(2,1)}) %all-gather.3.cloned.1.call-update) | async-done | bytes 1048592 | tf_op jit(solution)/shard_map/all_gather | solution.py:119
  34.9 1.5 fusion.14
  36.4 3.2 %fusion.23 = f32[256,768]{1,0:T(8,128)} fusion(bf16[2048,768]{1,0:T(8,128)(2,1)S(1)} %copy-done, bf16[1,256,2048]{2,1,0:T(8,128)(2,1)} %all-gather.3.cloned.1.call-done, f32[2048]{0:T(1024)} %param.24, f32[256]{0:T(256)S(1)} %add_rsqrt_fusion.1), kind=kOutput, calls=%fused_computation.51 | convolution fusion | flops 807403520 | bytes 4989952 | tf_op jit(solution)/shard_map/dot_general | solution.py:118
  39.6 1.3 reshape.405
  42.0 1.3 copy-done.9
  43.3 1.7 fusion
  45.4 1.9 fusion.1
  47.4 2.9 %fusion.7 = f32[4,256,128]{2,1,0:T(8,128)S(1)} fusion(f32[4,256,2048]{2,1,0:T(8,128)S(1)} %get-tuple-element.13, f32[4,256]{1,0:T(4,128)S(1)} %add.169, f32[4,256]{1,0:T(4,128)S(1)} %max.8, pred[4,2048]{1,0:T(4,128)(4,1)S(1)} %iota_compare_fusion.6, bf16[4,1,2048,256]{3,2,0,1:T(8,128)(2,1)S(1)} %bitcast.160), kind=kOutput, calls=%fused_computation.17 | convolution fusion | flops 547356672 | bytes 11026432 | tf_op jit(solution)/shard_map/vmap(vmap())/dot_general | solution.py:72
  50.8 0.7 fusion.36
  51.7 38.5 %all-reduce.1 = bf16[256,2048]{1,0:T(8,128)(2,1)S(1)} all-reduce(f32[256,2048]{1,0:T(8,128)S(1)} %fusion.29), channel_id=1, replica_groups=mesh['req'=32,'head'=4] {'head'}, use_global_device_ids=true, to_apply=%region_6.7 | all-reduce | flops 524288 | bytes 3145728 | tf_op jit(solution)/shard_map/psum | solution.py:136
  90.9 1.0 copy-done.3
  91.8 0.8 fusion.10
  93.1 65.8 %all_to_all.10 = bf16[128,8,2048]{2,1,0:T(8,128)(2,1)S(1)} all-to-all(bf16[128,8,2048]{2,1,0:T(8,128)(2,1)S(1)} %bitcast.149), channel_id=1, replica_groups=mesh['req'=32,'head'=4] {'req','head'}, dimensions={0} | all-to-all | bytes 8388608 | tf_op jit(solution)/shard_map/all_to_all | solution.py:170
  158.9 6.7 %fusion.2 = f32[1024,1408]{1,0:T(8,128)S(1)} fusion(bf16[1,2048,1408]{2,1,0:T(8,128)(2,1)S(1)} %bitcast.166, bf16[128,8,2048]{2,1,0:T(8,128)(2,1)S(1)} %all_to_all.10), kind=kOutput, calls=%fused_computation.8 | convolution fusion | flops 5905580032 | bytes 15728640 | tf_op jit(solution)/shard_map/dot_general | solution.py:85
  165.6 5.2 %convert_bitcast_fusion = bf16[128,8,2048]{2,1,0:T(8,128)(2,1)} fusion(bf16[1,704,2048]{2,1,0:T(8,128)(2,1)S(1)} %copy-done.22, f32[1024,1408]{1,0:T(8,128)S(1)} %fusion.2), kind=kOutput, calls=%fused_computation.16 | convolution fusion | flops 2959212544 | bytes 13369344 | tf_op jit(solution)/shard_map/dot_general | solution.py:88
  170.9 5.2 %all-to-all-start.1 = ((bf16[128,8,2048]{2,1,0:T(8,128)(2,1)}), bf16[128,8,2048]{2,1,0:T(8,128)(2,1)}, u32[]{:S(2)}, u32[]{:S(2)}) async-start(bf16[128,8,2048]{2,1,0:T(8,128)(2,1)} %convert_bitcast_fusion), calls=%async_computation.2 | async-start | bytes 8388608 | tf_op jit(solution)/shard_map/all_to_all | solution.py:172
  177.3 4.9 %convolution_convert_fusion.1 = bf16[256,2048]{1,0:T(8,128)(2,1)} fusion(bf16[352,2048]{1,0:T(8,128)(2,1)} %param.30, bf16[256,2048]{1,0:T(8,128)(2,1)S(1)} %copy-done.4, bf16[2048,352]{0,1:T(8,128)(2,1)} %param.29, f32[256,352]{0,1:T(8,128)S(1)} %fusion.83), kind=kOutput, calls=%fused_computation.27 | convolution fusion | flops 739262464 | bytes 5341184 | tf_op jit(solution)/shard_map/dot_general | solution.py:145
  182.7 2.9 %gather_fusion.1 = f32[384]{0:T(512)S(1)} fusion(f32[64,64]{1,0:T(8,128)S(1)} %fusion.41, s32[384]{0:T(512)S(1)} %reshape.425), kind=kCustom, calls=%fused_computation.1 | custom fusion | bytes 6144 | tf_op jit(solution)/shard_map/jit(take_along_axis)/gather | solution.py:155
  185.9 0.9 fusion.71
  188.3 49.2 %all-to-all-done.1 = bf16[128,8,2048]{2,1,0:T(8,128)(2,1)} async-done(((bf16[128,8,2048]{2,1,0:T(8,128)(2,1)}), bf16[128,8,2048]{2,1,0:T(8,128)(2,1)}, u32[]{:S(2)}, u32[]{:S(2)}) %all-to-all-start.1) | async-done | bytes 4194336 | tf_op jit(solution)/shard_map/all_to_all | solution.py:172
  237.5 3.3 %convert.24 = f32[64,2,8,2048]{3,2,1,0:T(8,128)S(1)} convert(bf16[64,2,8,2048]{3,2,1,0:T(8,128)(2,1)} %bitcast.26) | non-fusion elementwise | flops 2097152 | bytes 12582912 | tf_op jit(solution)/shard_map/convert_element_type | solution.py:175
  240.8 2.7 fusion.5
  243.5 7.3 %gather_fusion = f32[384,2048]{1,0:T(8,128)} fusion(f32[512,2048]{1,0:T(8,128)} %fusion.5, s32[1024]{0:T(1024)S(1)} %pad_clamp_fusion), kind=kCustom, calls=%fused_computation | custom fusion | bytes 6292992 | tf_op jit(solution)/shard_map/gather | solution.py:177
  250.7 4.8 %reshape.418 = f32[64,6,2048]{2,1,0:T(8,128)} reshape(f32[384,2048]{1,0:T(8,128)} %gather_fusion) | data formatting | bytes 6291456 | tf_op jit(solution)/shard_map/gather | solution.py:177
  255.6 4.5 %multiply_reduce_fusion = f32[64,2048]{1,0:T(8,128)} fusion(f32[64,6,2048]{2,1,0:T(8,128)} %reshape.418, f32[64,6]{1,0:T(8,128)S(1)} %copy.74), kind=kLoop, calls=%fused_computation.15 | loop fusion | flops 1441792 | bytes 3671552 | tf_op jit(solution)/shard_map/reduce_sum | solution.py:177
  260.1 2.0 fusion.35
  (116 shorter events, 11.4 us)
Async XLA Ops:
  7.2 29.2 %copy-start = (bf16[2048,768]{1,0:T(8,128)(2,1)S(1)}, bf16[2048,768]{1,0:T(8,128)(2,1)}, u32[]{:S(2)}) copy-start(bf16[2048,768]{1,0:T(8,128)(2,1)} %param.25) | copy-start | bytes 9437188
  7.2 8.2 %copy-start.15 = (s32[1,64,6]{1,0,2:T(1,128)S(1)}, s32[1,64,6]{1,0,2:T(1,128)}, u32[]{:S(2)}) copy-start(s32[1,64,6]{1,0,2:T(1,128)} %param.22) | copy-start | bytes 4612
  7.2 27.7 %all-gather.3.cloned.1.call-start = ((), (), s32[]{:S(2)}) async-start(), calls=%async_computation.4 | async-start | bytes 1310720 | tf_op jit(solution)/shard_map/all_gather | solution.py:119
  8.8 1.0 copy-start.10
  11.1 3.1 %copy-start.16 = (s32[384]{0:T(512)}, s32[384]{0:T(512)S(1)}, u32[]{:S(2)}) copy-start(s32[384]{0:T(512)S(1)} %fusion.58) | copy-start | bytes 4612
  15.4 0.9 copy-start.20
  39.6 1.5 copy-start.21
  40.9 2.5 copy-start.9
  41.0 9.2 %copy-start.5 = (f32[4,64,1,6,128]{4,1,0,3,2:T(8,128)}, f32[4,64,1,6,128]{4,1,0,3,2:T(8,128)S(1)}, u32[]{:S(2)}) copy-start(f32[4,64,1,6,128]{4,1,0,3,2:T(8,128)S(1)} %copy.105) | copy-start | bytes 2359300
  43.3 1.7 copy-start.13
  47.4 3.5 %copy-start.6 = (bf16[512,2048]{1,0:T(8,128)(2,1)S(1)}, bf16[512,2048]{1,0:T(8,128)(2,1)}, u32[]{:S(2)}) copy-start(bf16[512,2048]{1,0:T(8,128)(2,1)} %param.26) | copy-start | bytes 6291460
  50.3 1.3 copy-start.8
  51.6 39.0 %copy-start.18 = (f32[2048]{0:T(1024)S(1)}, f32[2048]{0:T(1024)}, u32[]{:S(2)}) copy-start(f32[2048]{0:T(1024)} %param.27) | copy-start | bytes 24580
  51.7 40.2 %copy-start.14 = (pred[64,512]{1,0:T(8,128)(4,1)S(1)}, pred[64,512]{1,0:T(8,128)(4,1)}, u32[]{:S(2)}) copy-start(pred[64,512]{1,0:T(8,128)(4,1)} %fusion.28) | copy-start | bytes 98308
  90.2 2.9 %copy-start.2 = (bf16[256,2048]{1,0:T(8,128)(2,1)}, bf16[256,2048]{1,0:T(8,128)(2,1)S(1)}, u32[]{:S(2)}) copy-start(bf16[256,2048]{1,0:T(8,128)(2,1)S(1)} %all-reduce.1) | copy-start | bytes 3145732
  90.8 1.0 copy-start.3
  92.6 66.4 %slice-start = ((s8[5767168]{0:T(1024)(128)(4,1)}), s8[4194304]{0:T(1024)(128)(4,1)S(1)}, s32[]{:S(2)}) async-start(s8[5767168]{0:T(1024)(128)(4,1)} %bitcast.165), calls=%async_computation.5 | async-start | bytes 8388608
  93.1 65.8 %slice-start.1 = ((s8[5767168]{0:T(1024)(128)(4,1)}), s8[1572864]{0:T(1024)(128)(4,1)S(1)}, s32[]{:S(2)}) async-start(s8[5767168]{0:T(1024)(128)(4,1)} %bitcast.165), calls=%async_computation.6 | async-start | bytes 3145728
  158.9 6.7 %copy-start.22 = (bf16[1,704,2048]{2,1,0:T(8,128)(2,1)S(1)}, bf16[1,704,2048]{2,1,0:T(8,128)(2,1)}, u32[]{:S(2)}) copy-start(bf16[1,704,2048]{2,1,0:T(8,128)(2,1)} %param.33) | copy-start | bytes 8650756
  170.8 5.5 %copy-start.17 = (s32[384]{0:T(512)S(1)}, s32[384]{0:T(512)}, u32[]{:S(2)}) copy-start(s32[384]{0:T(512)} %copy-done.16) | copy-start | bytes 4612
  170.8 5.6 %copy-start.11 = (s32[1,64,6]{2,1,0:T(8,128)S(1)}, s32[1,64,6]{2,1,0:T(8,128)}, u32[]{:S(2)}) copy-start(s32[1,64,6]{2,1,0:T(8,128)} %copy-done.10) | copy-start | bytes 4612
  170.8 5.8 %copy-start.23 = (s32[1,64]{1,0:T(1,128)S(1)}, s32[1,64]{1,0:T(1,128)}, u32[]{:S(2)}) copy-start(s32[1,64]{1,0:T(1,128)} %param.18) | copy-start | bytes 772
  170.8 5.8 %copy-start.19 = (s32[4,8]{1,0:T(4,128)S(1)}, s32[4,8]{1,0:T(4,128)}, u32[]{:S(2)}) copy-start(s32[4,8]{1,0:T(4,128)} %param.21) | copy-start | bytes 388
  170.9 5.9 %copy-start.4 = (bf16[256,2048]{1,0:T(8,128)(2,1)S(1)}, bf16[256,2048]{1,0:T(8,128)(2,1)}, u32[]{:S(2)}) copy-start(bf16[256,2048]{1,0:T(8,128)(2,1)} %copy-done.3) | copy-start | bytes 3145732
  170.9 5.9 %copy-start.7 = (bf16[2048,352]{0,1:T(8,128)(2,1)S(1)}, bf16[2048,352]{0,1:T(8,128)(2,1)}, u32[]{:S(2)}) copy-start(bf16[2048,352]{0,1:T(8,128)(2,1)} %param.28) | copy-start | bytes 4325380
  170.9 66.6 %all-to-all-start.1 = ((bf16[128,8,2048]{2,1,0:T(8,128)(2,1)}), bf16[128,8,2048]{2,1,0:T(8,128)(2,1)}, u32[]{:S(2)}, u32[]{:S(2)}) async-start(bf16[128,8,2048]{2,1,0:T(8,128)(2,1)} %convert_bitcast_fusion), calls=%async_computation.2 | async-start | bytes 8388608 | tf_op jit(solution)/shard_map/all_to_all | solution.py:172
  176.1 84.1 %reduce-scatter.2.cloned.1.call-start = ((), (), s32[]{:S(2)}) async-start(), calls=%async_computation.3 | async-start | bytes 1310720 | tf_op jit(solution)/shard_map/reduce_scatter | solution.py:144
  177.3 5.1 %copy-start.12 = (bf16[2048,64]{0,1:T(8,128)(2,1)S(1)}, bf16[2048,64]{0,1:T(8,128)(2,1)}, u32[]{:S(2)}) copy-start(bf16[2048,64]{0,1:T(8,128)(2,1)} %param.31) | copy-start | bytes 786436
  250.7 11.4 %copy-start.1 = (bf16[2048,768]{1,0:T(8,128)(2,1)S(1)}, bf16[2048,768]{1,0:T(8,128)(2,1)}, u32[]{:S(2)}) copy-start(bf16[2048,768]{1,0:T(8,128)(2,1)} %param.25) | copy-start | bytes 9437188
Sparse Core Ops, SparseCore 0:
  9.7 25.1 all-gather.2
  182.3 39.7 reduce-scatter.1
where the time goes:
time: 270 us; the launch traced here: 269 us
  blocking collectives  104 us (39%)
  waiting for transfers between devices  67.3 us (25%)
  matrix products  30.1 us (11%)
  local copies, waits for them, and re-layouts  24.8 us (9%)
  other arithmetic  22.3 us (8%)
  between operations  14.7 us (5%)
  starting transfers between devices  5.48 us (2%)
    all_to_all x1, blocking collectives, body(): lax.all_to_all(outgoing, ('req', 'head'), split_axis=0, concat_axis=0, ti...  65.8 us
    all_to_all x1, waiting for transfers between devices, body(): lax.all_to_all(partial_value, ('req', 'head'), split_axis=0, concat_axis=...  49.2 us
    psum x1, blocking collectives, body(): resid_all = lax.psum(term, 'head').astype(jnp.bfloat16)  38.5 us
    all_gather x1, waiting for transfers between devices, body(): lax.all_gather(own_rows, 'head', axis=0, tiled=True)  17.4 us
    gather x2, local copies, waits for them, and re-layouts, body(): routed = jnp.sum(gates[:, :, None] * expert_rows[target], axis=1)  12.1 us
    dot_general x1, matrix products, expert_half(): both = jnp.dot(rows, inner, preferred_element_type=jnp.float32)  6.65 us
  transfers between devices with their start and end apart: 3, of which 2 were waited for; matrix products, arithmetic and copies ran while one was open for 16% of the time, Pallas kernels for 0%

commit v1 on v0

v1 whole, which is shorter than its diff:
```python
import functools
import math

import jax
import jax.numpy as jnp
from jax import lax
from jax.experimental import pallas as pl
from jax.experimental.pallas import tpu as pltpu
from jax.sharding import PartitionSpec as P

EPSILON = 1e-06
ROPE_BASE = 10000.0
MESH = pl.DeviceIdType.MESH
NX, NY, NZ, NC = 4, 4, 4, 2
GROUP = NY * NZ * NC
VMEM = pl.BlockSpec(memory_space=pltpu.VMEM)


def rms_norm(values, gain):
    wide = values.astype(jnp.float32)
    power = jnp.mean(wide * wide, axis=-1, keepdims=True)
    return (wide * lax.rsqrt(power + EPSILON) * gain).astype(jnp.bfloat16)


def rotate(values, position):
    half = values.shape[-1] // 2
    frequency = ROPE_BASE ** (-jnp.arange(half, dtype=jnp.float32) / half)
    angle = position[..., None] * frequency
    cosine = jnp.cos(angle)
    sine = jnp.sin(angle)
    first = values[..., :half]
    second = values[..., half:]
    return jnp.concatenate(
        [first * cosine - second * sine, second * cosine + first * sine], axis=-1
    )


def ancestry(parents):
    nodes_count = parents.shape[-1]
    nodes = jnp.arange(nodes_count, dtype=jnp.int32)
    reach = (parents[..., :, None] == nodes).astype(jnp.bfloat16) + jnp.eye(
        nodes_count, dtype=jnp.bfloat16
    )
    for turn in range((nodes_count - 1).bit_length()):
        reach = jnp.minimum(
            jnp.einsum("rij,rjk->rik", reach, reach, preferred_element_type=jnp.float32), 1.0
        ).astype(jnp.bfloat16)
    reach = reach.astype(jnp.float32)
    depth = jnp.sum(reach, axis=-1) - 1.0
    return (reach, depth)


def head_group(projected, position, length, reach, cache_rows):
    group = projected.shape[0] - 2
    tree = projected.shape[1]
    head_dim = projected.shape[2]
    query = rotate(projected[:group], position).astype(jnp.bfloat16).reshape(group * tree, head_dim)
    key_new = rotate(projected[group], position).astype(jnp.bfloat16)
    value_new = projected[group + 1].astype(jnp.bfloat16)
    scale = 1.0 / math.sqrt(head_dim)
    cache_keys = cache_rows[:, :head_dim]
    cache_values = cache_rows[:, head_dim:]
    old_scores = (
        jnp.einsum("qd,kd->qk", query, cache_keys, preferred_element_type=jnp.float32) * scale
    )
    new_scores = jnp.einsum("qd,kd->qk", query, key_new, preferred_element_type=jnp.float32) * scale
    visible = jnp.arange(cache_rows.shape[0], dtype=jnp.int32) < length
    old_scores = jnp.where(visible[None, :], old_scores, -1e30)
    new_scores = jnp.where(jnp.tile(reach, (group, 1)) > 0.5, new_scores, -1e30)
    peak = jnp.maximum(
        jnp.max(old_scores, axis=-1, keepdims=True), jnp.max(new_scores, axis=-1, keepdims=True)
    )
    old_weights = jnp.exp(old_scores - peak)
    new_weights = jnp.exp(new_scores - peak)
    denominator = jnp.sum(old_weights, axis=-1, keepdims=True) + jnp.sum(
        new_weights, axis=-1, keepdims=True
    )
    old_probs = (old_weights / denominator).astype(jnp.bfloat16)
    new_probs = (new_weights / denominator).astype(jnp.bfloat16)
    mixed = jnp.dot(old_probs, cache_values, preferred_element_type=jnp.float32) + jnp.dot(
        new_probs, value_new, preferred_element_type=jnp.float32
    )
    mixed = (
        mixed.astype(jnp.bfloat16)
        .reshape(group, tree, head_dim)
        .transpose(1, 0, 2)
        .reshape(tree, group * head_dim)
    )
    return (mixed, jnp.concatenate([key_new, value_new], axis=-1))


def place():
    r = lax.axis_index("req")
    return r // (NY * NC), (r // NC) % NY, r % NC, lax.axis_index("head")


def device(z, y, c, x):
    return (z * (NY * NC) + y * NC + c, x)


def rendezvous(peers):
    barrier = pltpu.get_barrier_semaphore()
    for peer in peers:
        pl.semaphore_signal(barrier, inc=1, device_id=peer, device_id_type=MESH)
    pl.semaphore_wait(barrier, len(peers))


def remote(src, dst, send, recv, peer):
    return pltpu.make_async_remote_copy(
        src_ref=src, dst_ref=dst, send_sem=send, recv_sem=recv, device_id=peer, device_id_type=MESH
    )


def gather_kernel(rows_ref, table_ref, rows_out, table_out, send, recv, local):
    z, y, c, x = place()
    peers = [device(z, y, c, (x + d) % NX) for d in (1, 3, 2)]
    rendezvous(peers)
    copies = []
    for i, peer in enumerate(peers):
        copies.append(remote(table_ref, table_out.at[x], send.at[1, i], recv.at[1, i], peer))
        copies.append(remote(rows_ref, rows_out.at[x], send.at[0, i], recv.at[0, i], peer))
    for copy in copies:
        copy.start()
    own = [
        pltpu.make_async_copy(rows_ref, rows_out.at[x], local.at[0]),
        pltpu.make_async_copy(table_ref, table_out.at[x], local.at[1]),
    ]
    for copy in own:
        copy.start()
    for copy in own + copies:
        copy.wait()


def gather_rows(rows, table):
    return pl.pallas_call(
        gather_kernel,
        out_shape=(
            jax.ShapeDtypeStruct((NX,) + rows.shape, rows.dtype),
            jax.ShapeDtypeStruct((NX,) + table.shape, table.dtype),
        ),
        in_specs=[VMEM, VMEM],
        out_specs=(VMEM, VMEM),
        scratch_shapes=[
            pltpu.SemaphoreType.DMA((2, 3)),
            pltpu.SemaphoreType.DMA((2, 3)),
            pltpu.SemaphoreType.DMA((2,)),
        ],
        compiler_params=pltpu.CompilerParams(collective_id=1, has_side_effects=True),
        name="gather_rows",
    )(rows, table)


PIECES = 2


def resid_kernel(term_ref, own_ref, gain_ref, resid_out, normed_out, got, mine, send, recv, send2, recv2):
    z, y, c, x = place()
    peers = [(x + d) % NX for d in (1, 3, 2)]
    rendezvous([device(z, y, c, p) for p in peers])
    rows = own_ref.shape[0] // PIECES
    first = []
    for piece in range(PIECES):
        part = pl.ds(piece * rows, rows)
        for i, p in enumerate(peers):
            copy = remote(
                term_ref.at[p, part], got.at[i, part], send.at[piece, i], recv.at[piece, i],
                device(z, y, c, p),
            )
            copy.start()
            first.append(copy)
    second = []
    for piece in range(PIECES):
        part = pl.ds(piece * rows, rows)
        for i in range(3):
            first[piece * 3 + i].wait_recv()
        total = own_ref[part]
        for i in range(3):
            total = total + got[i, part].astype(jnp.float32)
        resid = total.astype(jnp.bfloat16)
        resid_out[part] = resid
        normed = rms_norm(resid, gain_ref[...])
        mine[part] = normed
        normed_out[x, part] = normed
        for i, p in enumerate(peers):
            copy = remote(
                mine.at[part], normed_out.at[x, part], send2.at[piece, i], recv2.at[piece, i],
                device(z, y, c, p),
            )
            copy.start()
            second.append(copy)
    for copy in first:
        copy.wait_send()
    for copy in second:
        copy.wait()


def resid_rows(term, own, gain):
    rows, width = own.shape
    sem = pltpu.SemaphoreType.DMA((PIECES, 3))
    return pl.pallas_call(
        resid_kernel,
        out_shape=(
            jax.ShapeDtypeStruct((rows, width), jnp.bfloat16),
            jax.ShapeDtypeStruct((NX, rows, width), jnp.bfloat16),
        ),
        in_specs=[VMEM] * 3,
        out_specs=(VMEM, VMEM),
        scratch_shapes=[
            pltpu.VMEM((3, rows, width), jnp.bfloat16),
            pltpu.VMEM((rows, width), jnp.bfloat16),
            sem, sem, sem, sem,
        ],
        compiler_params=pltpu.CompilerParams(collective_id=2, has_side_effects=True),
        name="resid_rows",
    )(term, own, gain)


def exchange_kernel(src, out, mid_y, mid_z, send1, recv1, send2, recv2, local):
    z, y, c, x = place()
    half = src.shape[-1] // 2
    left, right = pl.ds(0, half), pl.ds(half, half)
    order = (1, 3, 2)
    peers = [device(z, (y + d) % NY, (c + e) % NC, x) for d in order for e in range(NC)]
    peers += [device((z + d) % NZ, y, (c + e) % NC, x) for d in order for e in range(NC)]
    peers += [device(z, y, 1 - c, x)]
    rendezvous(peers)
    copies = []
    arrive_y, arrive_z = {}, {}
    for d in order:
        yd, zd = (y + d) % NY, (z + d) % NZ
        copy = remote(
            src.at[:, yd, :, :, left], mid_y.at[d - 1], send1.at[0, d - 1], recv1.at[0, d - 1],
            device(z, yd, c, x),
        )
        copy.start()
        arrive_y[d] = copy
        copy = remote(
            src.at[zd, :, :, :, right], mid_z.at[d - 1], send1.at[1, d - 1], recv1.at[1, d - 1],
            device(zd, y, c, x),
        )
        copy.start()
        arrive_z[d] = copy

    for d in (0,) + order:
        ys, zs = (y - d) % NY, (z - d) % NZ
        if d:
            arrive_y[d].wait_recv()
            arrive_z[d].wait_recv()
        for f in order + (0,):
            yf, zf = (y + f) % NY, (z + f) % NZ
            for e in range(NC):
                ce = (c + e) % NC
                slot = (d * 4 + f) * NC + e
                a = src.at[zf, y, ce, :, left] if d == 0 else mid_y.at[d - 1, zf, ce]
                b = src.at[z, yf, ce, :, right] if d == 0 else mid_z.at[d - 1, yf, ce]
                to_a, to_b = out.at[z, ys, c, :, left], out.at[zs, y, c, :, right]
                if f == 0 and e == 0:
                    pair = [
                        pltpu.make_async_copy(a, to_a, local.at[0, d]),
                        pltpu.make_async_copy(b, to_b, local.at[1, d]),
                    ]
                else:
                    pair = [
                        remote(a, to_a, send2.at[0, slot], recv2.at[0, slot], device(zf, y, ce, x)),
                        remote(b, to_b, send2.at[1, slot], recv2.at[1, slot], device(z, yf, ce, x)),
                    ]
                for copy in pair:
                    copy.start()
                copies += pair
    for d in order:
        arrive_y[d].wait_send()
        arrive_z[d].wait_send()
    for copy in copies:
        copy.wait()


def exchange(blocks, identifier):
    rows, width = blocks.shape[-2:]
    return pl.pallas_call(
        exchange_kernel,
        out_shape=jax.ShapeDtypeStruct(blocks.shape, blocks.dtype),
        in_specs=[VMEM],
        out_specs=VMEM,
        scratch_shapes=[
            pltpu.VMEM((3, NZ, NC, rows, width // 2), blocks.dtype),
            pltpu.VMEM((3, NY, NC, rows, width // 2), blocks.dtype),
            pltpu.SemaphoreType.DMA((2, 3)),
            pltpu.SemaphoreType.DMA((2, 3)),
            pltpu.SemaphoreType.DMA((2, 32)),
            pltpu.SemaphoreType.DMA((2, 32)),
            pltpu.SemaphoreType.DMA((2, 4)),
        ],
        compiler_params=pltpu.CompilerParams(collective_id=identifier, has_side_effects=True),
        name="exchange",
    )(blocks)


def final_kernel(part_ref, own_ref, live_ref, out, got, send, recv):
    z, y, c, x = place()
    peers = [(x + d) % NX for d in (1, 3, 2)]
    rendezvous([device(z, y, c, p) for p in peers])
    copies = [
        remote(part_ref.at[p], got.at[i], send.at[i], recv.at[i], device(z, y, c, p))
        for i, p in enumerate(peers)
    ]
    for copy in copies:
        copy.start()
    for copy in copies:
        copy.wait()
    total = own_ref[...]
    for i in range(3):
        total = total + got[i].astype(jnp.float32)
    out[...] = jnp.where(live_ref[...] == 1, total, 0.0).astype(jnp.bfloat16)


def final_rows(part, own, live):
    rows, width = own.shape
    return pl.pallas_call(
        final_kernel,
        out_shape=jax.ShapeDtypeStruct((rows, width), jnp.bfloat16),
        in_specs=[VMEM] * 3,
        out_specs=VMEM,
        scratch_shapes=[
            pltpu.VMEM((3, rows, width), jnp.bfloat16),
            pltpu.SemaphoreType.DMA((3,)),
            pltpu.SemaphoreType.DMA((3,)),
        ],
        compiler_params=pltpu.CompilerParams(collective_id=5, has_side_effects=True),
        name="final_rows",
    )(part, own, live)


def expert_half(rows, inner, outer):
    both = jnp.dot(rows, inner, preferred_element_type=jnp.float32)
    half = inner.shape[1] // 2
    hidden = (jax.nn.silu(both[:, :half]) * both[:, half:]).astype(jnp.bfloat16)
    return jnp.dot(hidden, outer, preferred_element_type=jnp.float32).astype(jnp.bfloat16)


def body(
    tokens,
    live,
    parents,
    lengths,
    accepted,
    routes,
    cache,
    attn_gain,
    w_qkv,
    w_out,
    ffn_gain,
    shared_gate,
    shared_up,
    shared_down,
    router,
    expert_in,
    expert_out,
):
    tree, width = tokens.shape[1:]
    own_rows = tokens[0]
    x = lax.axis_index("head")
    local_heads = cache.shape[1]
    head_dim = cache.shape[3] // 2
    group = w_qkv.shape[1] // (local_heads * head_dim) - 2
    top_count = routes.shape[2]
    expert_count = router.shape[1]
    capacity = 4 * tree * top_count // (3 * expert_count)

    table = jnp.pad(routes[0].T, ((0, 8 - top_count), (0, 128 - tree)))
    normed_all, table_all = gather_rows(rms_norm(own_rows, attn_gain), table)

    projected = jnp.dot(
        normed_all.reshape(NX * tree, width), w_qkv, preferred_element_type=jnp.float32
    )
    projected = projected.reshape(NX, tree, local_heads, group + 2, head_dim).transpose(
        0, 2, 3, 1, 4
    )
    reach, depth = ancestry(parents)
    positions = lengths[:, None].astype(jnp.float32) + depth
    inner_map = jax.vmap(head_group, in_axes=(0, None, None, None, 0))
    mixed, fresh = jax.vmap(inner_map)(projected, positions, lengths, reach, cache)
    mixed = mixed.transpose(0, 2, 1, 3).reshape(NX * tree, local_heads * group * head_dim)
    accepted_kv = jnp.take_along_axis(fresh, accepted[:, None, :, None], axis=2)

    term = jnp.dot(mixed, w_out, preferred_element_type=jnp.float32).reshape(NX, tree, width)
    own_term = lax.dynamic_index_in_dim(term, x, 0, keepdims=False) + own_rows.astype(jnp.float32)
    resid, normed2 = resid_rows(term.astype(jnp.bfloat16), own_term, ffn_gain[None])
    normed2 = normed2.reshape(NX * tree, width)

    choose = table_all[:, :top_count, :tree]
    named = jnp.any(
        choose[:, :, :, None] == jnp.arange(expert_count, dtype=jnp.int32), axis=1
    ).astype(jnp.float32)
    earlier = jnp.tril(jnp.ones((tree, tree), jnp.bfloat16), -1)
    rank = jnp.einsum(
        "ts,rse->rte", earlier, named.astype(jnp.bfloat16), preferred_element_type=jnp.float32
    )
    logits = jnp.dot(normed2, router, preferred_element_type=jnp.float32)
    picked = jax.nn.sigmoid(logits).reshape(NX, tree, expert_count) * named
    gates = picked / jnp.sum(picked, axis=-1, keepdims=True)
    pair = x // 2
    slot = jnp.where(named > 0.5, rank, -1.0)

    def of_pair(values):
        values = values.reshape(NX, tree, GROUP, expert_count // GROUP)
        return jnp.where(pair == 0, values[..., 0], values[..., 1])

    slot = of_pair(slot)
    gates = of_pair(gates)
    same = jnp.arange(NX)[:, None, None, None, None] == jnp.arange(NX)[:, None]
    taken = (slot[:, :, :, None, None] == jnp.arange(capacity, dtype=jnp.float32)) & same
    taken = taken.reshape(NX * tree, GROUP * NX * capacity)
    weight = jnp.broadcast_to(
        gates[:, :, :, None, None], (NX, tree, GROUP, NX, capacity)
    ).reshape(NX * tree, GROUP * NX * capacity)
    weight = jnp.where(taken, weight, 0.0)
    weight_high = weight.astype(jnp.bfloat16)
    weight_low = (weight - weight_high.astype(jnp.float32)).astype(jnp.bfloat16)
    outgoing = lax.dot_general(
        taken.astype(jnp.bfloat16), normed2, (((0,), (0,)), ((), ())),
        preferred_element_type=jnp.float32,
    ).astype(jnp.bfloat16)
    blocks = (NZ, NY, NC, NX * capacity, width)
    received = exchange(outgoing.reshape(blocks), 3)
    half_out = expert_half(received.reshape(-1, width), expert_in[0], expert_out[0])
    returned = exchange(half_out.reshape(blocks), 4).reshape(-1, width)

    gated = jax.nn.silu(jnp.dot(normed2, shared_gate, preferred_element_type=jnp.float32))
    hidden = (gated * jnp.dot(normed2, shared_up, preferred_element_type=jnp.float32)).astype(
        jnp.bfloat16
    )
    part = (
        jnp.dot(hidden, shared_down, preferred_element_type=jnp.float32)
        + jnp.dot(weight_high, returned, preferred_element_type=jnp.float32)
        + jnp.dot(weight_low, returned, preferred_element_type=jnp.float32)
    ).reshape(NX, tree, width)
    own_part = lax.dynamic_index_in_dim(part, x, 0, keepdims=False) + resid.astype(jnp.float32)
    hidden_out = final_rows(part.astype(jnp.bfloat16), own_part, live.reshape(tree, 1))
    return (hidden_out[None], accepted_kv)


def solution(mesh):
    in_specs = (
        P(("req", "head"), None, None),
        P(("req", "head"), None),
        P("req", None),
        P("req"),
        P("req", None),
        P(("req", "head"), None, None),
        P("req", "head", None, None),
        P(),
        P(None, "head"),
        P("head", None),
        P(),
        P(None, "head"),
        P(None, "head"),
        P("head", None),
        P(),
        P(("req", "head"), None, None),
        P(("req", "head"), None, None),
    )
    out_specs = (P(("req", "head"), None, None), P("req", "head", None, None))
    return jax.shard_map(body, mesh=mesh, in_specs=in_specs, out_specs=out_specs, check_vma=False)
```

time: 270 us -> 284 us (1.052)
  Pallas kernels: 0 us -> 178 us
  blocking collectives: 104 us -> 0 us
  waiting for transfers between devices: 67.3 us -> 0 us
  matrix products: 30.1 us -> 57.8 us
  between operations: 14.7 us -> 1.09 us
  starting transfers between devices: 5.48 us -> 0 us
    pallas_call x0 -> x5, Pallas kernels: none -> 178 us  [the longest x2 115 us: exchange(): pl.pallas_call(exchange_kernel, out_shape=jax.ShapeDtypeStruct(blocks.sha...]
    all_to_all x1 -> x0, blocking collectives: 65.8 us -> none  [body(): lax.all_to_all(outgoing, ('req', 'head'), split_axis=0, concat_axis=0, ti...]
    all_to_all x1 -> x0, waiting for transfers between devices: 49.2 us -> none  [body(): lax.all_to_all(partial_value, ('req', 'head'), split_axis=0, concat_axis=...]
    psum x1 -> x0, blocking collectives: 38.5 us -> none  [body(): resid_all = lax.psum(term, 'head').astype(jnp.bfloat16)]
    dot_general x12 -> x11, matrix products: 8.21 us -> 26.8 us  [the longest x1 4.95 us: body(): jnp.dot(weight_high, returned, preferred_element_type=jnp.float32)]
    all_gather x1 -> x0, waiting for transfers between devices: 17.4 us -> none  [body(): lax.all_gather(own_rows, 'head', axis=0, tiled=True)]
    gather x6 -> x0, local copies, waits for them, and re-layouts: 15.3 us -> none  [the longest x2 12.1 us: body(): routed = jnp.sum(gates[:, :, None] * expert_rows[target], axis=1)]
    all_to_all x1 -> x0, starting transfers between devices: 5.18 us -> none  [body(): lax.all_to_all(partial_value, ('req', 'head'), split_axis=0, concat_axis=...]
  transfers between devices with their start and end apart: 3 -> 0, of which waited for: 2 -> 0; matrix products, arithmetic and copies ran while one was open for 16% -> 0% of each run, Pallas kernels for 0% -> 0%
where the time goes in v1:
time: 284 us; the launch traced here: 283 us
  Pallas kernels  178 us (63%)
  matrix products  57.8 us (20%)
  local copies, waits for them, and re-layouts  24.1 us (8%)
  other arithmetic  22.3 us (8%)
    pallas_call x2, Pallas kernels, exchange(): pl.pallas_call(exchange_kernel, out_shape=jax.ShapeDtypeStruct(blocks.sha...  115 us
    pallas_call x1, Pallas kernels, resid_rows(): pl.pallas_call(resid_kernel, out_shape=(jax.ShapeDtypeStruct((rows, width...  27.3 us
    pallas_call x1, Pallas kernels, gather_rows(): pl.pallas_call(gather_kernel, out_shape=(jax.ShapeDtypeStruct((NX,) + row...  18.1 us
    pallas_call x1, Pallas kernels, final_rows(): pl.pallas_call(final_kernel, out_shape=jax.ShapeDtypeStruct((rows, width)...  17.3 us
    dot_general x1, matrix products, expert_half(): both = jnp.dot(rows, inner, preferred_element_type=jnp.float32)  10.4 us
    unnamed x37, local copies, waits for them, and re-layouts  7.36 us
    dot_general x1, matrix products, body(): jnp.dot(hidden, shared_down, preferred_element_type=jnp.float32)  6.82 us

profile of v1, /device:TPU:1, one launch (start us, length us, event | category | flops | bytes accessed | tf_op | source)
XLA Modules:
  0.0 283.3 jit_solution(13708669667681438824)
XLA Ops:
  1.9 1.8 fusion.32.rows_ref
  5.0 18.1 %gather_rows.1 = (bf16[4,64,2048]{2,1,0:T(8,128)(2,1)}, s32[4,8,128]{2,1,0:T(8,128)}) custom-call(bf16[64,2048]{1,0:T(8,128)(2,1)} %fusion.32.rows_ref, s32[8,128]{1,0:T(8,128)} %pad.4.table_ref), custom_call_target="tpu_custom_call" | custom-call | tf_op jit(solution)/shard_map/gather_rows/pallas_call | solution.py:135
  23.1 4.7 %copy.58 = bf16[2048,768]{0,1:T(8,128)(2,1)} copy(bf16[2048,768]{1,0:T(8,128)(2,1)} %param.25) | data formatting | bytes 6291456 | tf_op args[8]
  27.7 4.1 %convolution_bitcast_fusion = f32[4,1,6,64,128]{4,3,2,0,1:T(8,128)} fusion(bf16[6,128,2048,1]{2,1,0,3:T(8,128)(2,1)} %bitcast.140, bf16[4,64,2048]{2,1,0:T(8,128)(2,1)} %get-tuple-element.6), kind=kOutput, calls=%fused_computation.25 | convolution fusion | flops 805306368 | bytes 4980736 | tf_op jit(solution)/shard_map/dot_general | solution.py:372
  34.2 1.5 subtract_convert_fusion
  37.3 1.6 broadcast_compare_fusion
  40.3 1.5 tile.2
  41.8 1.8 gt.16
  44.9 3.2 %fusion = (f32[4,256]{1,0:T(4,128)S(1)}, f32[4,256,2048]{2,1,0:T(8,128)S(1)}) fusion(pred[4,2048]{1,0:T(4,128)(4,1)S(1)} %iota_compare_fusion.5, bf16[4,1,2048,256]{3,2,0,1:T(8,128)(2,1)} %bitcast.146, bf16[4,256,64]{2,1,0:T(8,128)(2,1)S(1)} %bitcast.144, bf16[4,256,64]{2,1,0:T(8,128)(2,1)S(1)} %bitcast.142), kind=kOutput, calls=%fused_computation.4 | convolution fusion | flops 543685632 | bytes 10760192 | tf_op jit(solution)/shard_map/vmap(vmap(qd,kd->qk))/dot_general | solution.py:64
  48.2 1.9 fusion.1
  50.3 3.1 %fusion.4 = f32[4,256,128]{2,1,0:T(8,128)S(1)} fusion(f32[4,256,2048]{2,1,0:T(8,128)S(1)} %get-tuple-element.19, f32[4,256]{1,0:T(4,128)S(1)} %add.111, f32[4,256]{1,0:T(4,128)S(1)} %max.8, pred[4,2048]{1,0:T(4,128)(4,1)S(1)} %iota_compare_fusion.5, bf16[4,1,2048,256]{3,2,0,1:T(8,128)(2,1)S(1)} %bitcast.147), kind=kOutput, calls=%fused_computation.8 | convolution fusion | flops 547356672 | bytes 11026432 | tf_op jit(solution)/shard_map/vmap(vmap())/dot_general | solution.py:80
  55.7 4.1 %fusion.87 = (bf16[4,64,2048]{2,1,0:T(8,128)(2,1)}, f32[4,64,2048]{2,1,0:T(8,128)}) fusion(bf16[4,64,512]{2,1,0:T(8,128)(2,1)} %dot_general.85, bf16[512,2048]{1,0:T(8,128)(2,1)} %param.26), kind=kOutput, calls=%fused_computation.145 | convolution fusion | flops 537395200 | bytes 5505024 | tf_op jit(solution)/shard_map/dot_general | solution.py:385
  59.7 1.9 convert_add_fusion.own_ref
  61.6 27.3 %resid_rows.1 = (bf16[64,2048]{1,0:T(8,128)(2,1)}, bf16[4,64,2048]{2,1,0:T(8,128)(2,1)}) custom-call(bf16[4,64,2048]{2,1,0:T(8,128)(2,1)} %get-tuple-element.22.term_ref, f32[64,2048]{1,0:T(8,128)} %convert_add_fusion.own_ref, f32[1,2048]{1,0:T(1,128)} %bitcast.158), custom_call_target="tpu_custom_call" | custom-call | tf_op jit(solution)/shard_map/resid_rows/pallas_call | solution.py:200
  89.3 1.7 select_reduce_fusion
  93.4 1.6 and.54
  95.0 4.5 %convolution_convert_fusion.1 = bf16[1024,2048]{1,0:T(8,128)(2,1)} fusion(pred[256,1024]{0,1:T(32,128)(4,1)} %and.54, bf16[256,2048]{1,0:T(8,128)(2,1)} %bitcast.133), kind=kOutput, calls=%fused_computation.10 | convolution fusion | flops 1075838976 | bytes 5505024 | tf_op jit(solution)/shard_map/dot_general | solution.py:419
  99.5 60.8 %exchange.2 = bf16[4,4,2,32,2048]{4,3,2,1,0:T(8,128)(2,1)} custom-call(bf16[4,4,2,32,2048]{4,3,2,1,0:T(8,128)(2,1)} %bitcast.129), custom_call_target="tpu_custom_call" | custom-call | tf_op jit(solution)/shard_map/exchange/pallas_call | solution.py:279
  160.3 10.4 %fusion.2 = f32[1024,1408]{1,0:T(8,128)S(1)} fusion(bf16[1024,2048]{1,0:T(8,128)(2,1)} %bitcast.138, bf16[1,2048,1408]{2,1,0:T(8,128)(2,1)} %param.32), kind=kOutput, calls=%fused_computation.6 | convolution fusion | flops 5905580032 | bytes 15728640 | tf_op jit(solution)/shard_map/dot_general | solution.py:334
  170.8 5.2 %convolution_convert_fusion = bf16[1024,2048]{1,0:T(8,128)(2,1)} fusion(bf16[1,704,2048]{2,1,0:T(8,128)(2,1)S(1)} %copy-done, f32[1024,1408]{1,0:T(8,128)S(1)} %fusion.2), kind=kOutput, calls=%fused_computation.9 | convolution fusion | flops 2959212544 | bytes 13369344 | tf_op jit(solution)/shard_map/dot_general | solution.py:337
  176.0 54.5 %exchange.3 = bf16[4,4,2,32,2048]{4,3,2,1,0:T(8,128)(2,1)} custom-call(bf16[4,4,2,32,2048]{4,3,2,1,0:T(8,128)(2,1)} %bitcast.139), custom_call_target="tpu_custom_call" | custom-call | tf_op jit(solution)/shard_map/exchange/pallas_call | solution.py:279
  230.6 1.7 select_convert_fusion
  232.3 2.7 convert_element_type.183
  235.0 4.9 %fusion.89 = f32[256,2048]{1,0:T(8,128)} fusion(bf16[256,1024]{0,1:T(8,128)(2,1)} %convert_element_type.183, bf16[1024,2048]{1,0:T(8,128)(2,1)} %bitcast.136), kind=kOutput, calls=%fused_computation.147 | convolution fusion | flops 1073741824 | bytes 6815744 | tf_op jit(solution)/shard_map/dot_general | solution.py:434
  240.0 1.8 fusion.8
  241.8 2.1 convert_element_type.189
  243.9 4.9 %fusion.90 = f32[256,2048]{1,0:T(8,128)} fusion(bf16[256,1024]{0,1:T(8,128)(2,1)S(1)} %convert_element_type.189, bf16[1024,2048]{1,0:T(8,128)(2,1)} %bitcast.137), kind=kOutput, calls=%fused_computation.148 | convolution fusion | flops 1073741824 | bytes 6815744 | tf_op jit(solution)/shard_map/dot_general | solution.py:435
  249.5 6.8 %fusion.7 = f32[256,2048]{1,0:T(8,128)} fusion(f32[256,2048]{1,0:T(8,128)} %fusion.90, f32[256,2048]{1,0:T(8,128)} %fusion.89, bf16[352,2048]{1,0:T(8,128)(2,1)} %param.30, bf16[256,2048]{1,0:T(8,128)(2,1)} %bitcast.134, bf16[2048,352]{0,1:T(8,128)(2,1)} %param.29, f32[256,352]{0,1:T(8,128)S(1)} %fusion.88), kind=kOutput, calls=%fused_computation.15 | convolution fusion | flops 739786752 | bytes 10584064 | tf_op jit(solution)/shard_map/dot_general | solution.py:433
  256.3 2.0 bitcast_add_fusion.own_ref
  258.3 2.7 convert_element_type.190.part_ref
  261.8 17.3 %final_rows.1 = bf16[64,2048]{1,0:T(8,128)(2,1)} custom-call(bf16[4,64,2048]{2,1,0:T(8,128)(2,1)} %convert_element_type.190.part_ref, f32[64,2048]{1,0:T(8,128)} %bitcast_add_fusion.own_ref, s32[64,1]{1,0:T(8,128)} %copy.75.live_ref), custom_call_target="tpu_custom_call" | custom-call | tf_op jit(solution)/shard_map/final_rows/pallas_call | solution.py:318
  281.6 1.7 copy.95
  (81 shorter events, 18.2 us)
Async XLA Ops:
  0.6 170.1 %copy-start = (bf16[1,704,2048]{2,1,0:T(8,128)(2,1)S(1)}, bf16[1,704,2048]{2,1,0:T(8,128)(2,1)}, u32[]{:S(2)}) copy-start(bf16[1,704,2048]{2,1,0:T(8,128)(2,1)} %param.33) | copy-start | bytes 8650756
  27.7 4.1 %copy-start.16 = (s32[4,64]{1,0:T(4,128)S(1)}, s32[4,64]{1,0:T(4,128)}, u32[]{:S(2)}) copy-start(s32[4,64]{1,0:T(4,128)} %param.19) | copy-start | bytes 3076
  27.7 5.9 %copy-start.14 = (s32[4]{0:T(128)S(1)}, s32[4]{0:T(128)}, u32[]{:S(2)}) copy-start(s32[4]{0:T(128)} %param.20) | copy-start | bytes 52
  37.2 10.8 %copy-start.5 = (bf16[4,1,64,64]{3,2,0,1:T(8,128)(2,1)}, bf16[4,1,64,64]{3,2,0,1:T(8,128)(2,1)S(1)}, u32[]{:S(2)}) copy-start(bf16[4,1,64,64]{3,2,0,1:T(8,128)(2,1)S(1)} %get-tuple-element.12) | copy-start | bytes 98308
  37.2 10.8 %copy-start.7 = (bf16[4,1,64,64]{3,2,0,1:T(8,128)(2,1)}, bf16[4,1,64,64]{3,2,0,1:T(8,128)(2,1)S(1)}, u32[]{:S(2)}) copy-start(bf16[4,1,64,64]{3,2,0,1:T(8,128)(2,1)S(1)} %get-tuple-element.13) | copy-start | bytes 98308
  48.1 2.2 copy-start.4
  54.8 4.9 %copy-start.2 = (bf16[1,64,2048]{2,1,0:T(8,128)(2,1)S(1)}, bf16[1,64,2048]{2,1,0:T(8,128)(2,1)}, u32[]{:S(2)}) copy-start(bf16[1,64,2048]{2,1,0:T(8,128)(2,1)} %param.17) | copy-start | bytes 786436
  55.6 33.2 %copy-start.11 = (s32[4,8,128]{2,1,0:T(8,128)S(1)}, s32[4,8,128]{2,1,0:T(8,128)}, u32[]{:S(2)}) copy-start(s32[4,8,128]{2,1,0:T(8,128)} %get-tuple-element.8) | copy-start | bytes 49156
  55.7 33.6 %copy-start.15 = (bf16[2048,64]{0,1:T(8,128)(2,1)S(1)}, bf16[2048,64]{0,1:T(8,128)(2,1)}, u32[]{:S(2)}) copy-start(bf16[2048,64]{0,1:T(8,128)(2,1)} %param.31) | copy-start | bytes 786436
  176.0 54.5 %copy-start.10 = (f32[4,64,32,1]{1,3,2,0:T(1,128)S(1)}, f32[4,64,32,1]{1,3,2,0:T(1,128)}, u32[]{:S(2)}) copy-start(f32[4,64,32,1]{1,3,2,0:T(1,128)} %get-tuple-element.26) | copy-start | bytes 98308
  243.9 5.0 %copy-start.1 = (bf16[4,64,2048]{2,1,0:T(8,128)(2,1)S(1)}, bf16[4,64,2048]{2,1,0:T(8,128)(2,1)}, u32[]{:S(2)}) copy-start(bf16[4,64,2048]{2,1,0:T(8,128)(2,1)} %get-tuple-element.7) | copy-start | bytes 3145732
  243.9 5.0 %copy-start.3 = (bf16[2048,352]{0,1:T(8,128)(2,1)S(1)}, bf16[2048,352]{0,1:T(8,128)(2,1)}, u32[]{:S(2)}) copy-start(bf16[2048,352]{0,1:T(8,128)(2,1)} %param.28) | copy-start | bytes 4325380
  249.5 6.8 %copy-start.9 = (bf16[64,2048]{1,0:T(8,128)(2,1)S(1)}, bf16[64,2048]{1,0:T(8,128)(2,1)}, u32[]{:S(2)}) copy-start(bf16[64,2048]{1,0:T(8,128)(2,1)} %get-tuple-element.9) | copy-start | bytes 786436
  256.3 4.7 %copy-start.13 = (s32[1,64]{1,0:T(1,128)S(1)}, s32[1,64]{1,0:T(1,128)}, u32[]{:S(2)}) copy-start(s32[1,64]{1,0:T(1,128)} %param.18) | copy-start | bytes 772
  256.3 23.7 %copy-start.6 = (bf16[4,1,64,64]{3,2,0,1:T(8,128)(2,1)S(1)}, bf16[4,1,64,64]{3,2,0,1:T(8,128)(2,1)}, u32[]{:S(2)}) copy-start(bf16[4,1,64,64]{3,2,0,1:T(8,128)(2,1)} %copy-done.5) | copy-start | bytes 98308
  256.3 23.7 %copy-start.8 = (bf16[4,1,64,64]{3,2,0,1:T(8,128)(2,1)S(1)}, bf16[4,1,64,64]{3,2,0,1:T(8,128)(2,1)}, u32[]{:S(2)}) copy-start(bf16[4,1,64,64]{3,2,0,1:T(8,128)(2,1)} %copy-done.7) | copy-start | bytes 98308
  256.3 23.8 %copy-start.12 = (s32[4,8]{1,0:T(4,128)S(1)}, s32[4,8]{1,0:T(4,128)}, u32[]{:S(2)}) copy-start(s32[4,8]{1,0:T(4,128)} %param.21) | copy-start | bytes 388

commit v2 on v1

--- a/solution.py
+++ b/solution.py
@@ -22,73 +22,6 @@
     return (wide * lax.rsqrt(power + EPSILON) * gain).astype(jnp.bfloat16)
 
 
-def rotate(values, position):
-    half = values.shape[-1] // 2
-    frequency = ROPE_BASE ** (-jnp.arange(half, dtype=jnp.float32) / half)
-    angle = position[..., None] * frequency
-    cosine = jnp.cos(angle)
-    sine = jnp.sin(angle)
-    first = values[..., :half]
-    second = values[..., half:]
-    return jnp.concatenate(
-        [first * cosine - second * sine, second * cosine + first * sine], axis=-1
-    )
-
-
-def ancestry(parents):
-    nodes_count = parents.shape[-1]
-    nodes = jnp.arange(nodes_count, dtype=jnp.int32)
-    reach = (parents[..., :, None] == nodes).astype(jnp.bfloat16) + jnp.eye(
-        nodes_count, dtype=jnp.bfloat16
-    )
-    for turn in range((nodes_count - 1).bit_length()):
-        reach = jnp.minimum(
-            jnp.einsum("rij,rjk->rik", reach, reach, preferred_element_type=jnp.float32), 1.0
-        ).astype(jnp.bfloat16)
-    reach = reach.astype(jnp.float32)
-    depth = jnp.sum(reach, axis=-1) - 1.0
-    return (reach, depth)
-
-
-def head_group(projected, position, length, reach, cache_rows):
-    group = projected.shape[0] - 2
-    tree = projected.shape[1]
-    head_dim = projected.shape[2]
-    query = rotate(projected[:group], position).astype(jnp.bfloat16).reshape(group * tree, head_dim)
-    key_new = rotate(projected[group], position).astype(jnp.bfloat16)
-    value_new = projected[group + 1].astype(jnp.bfloat16)
-    scale = 1.0 / math.sqrt(head_dim)
-    cache_keys = cache_rows[:, :head_dim]
-    cache_values = cache_rows[:, head_dim:]
-    old_scores = (
-        jnp.einsum("qd,kd->qk", query, cache_keys, preferred_element_type=jnp.float32) * scale
-    )
-    new_scores = jnp.einsum("qd,kd->qk", query, key_new, preferred_element_type=jnp.float32) * scale
-    visible = jnp.arange(cache_rows.shape[0], dtype=jnp.int32) < length
-    old_scores = jnp.where(visible[None, :], old_scores, -1e30)
-    new_scores = jnp.where(jnp.tile(reach, (group, 1)) > 0.5, new_scores, -1e30)
-    peak = jnp.maximum(
-        jnp.max(old_scores, axis=-1, keepdims=True), jnp.max(new_scores, axis=-1, keepdims=True)
-    )
-    old_weights = jnp.exp(old_scores - peak)
-    new_weights = jnp.exp(new_scores - peak)
-    denominator = jnp.sum(old_weights, axis=-1, keepdims=True) + jnp.sum(
-        new_weights, axis=-1, keepdims=True
-    )
-    old_probs = (old_weights / denominator).astype(jnp.bfloat16)
-    new_probs = (new_weights / denominator).astype(jnp.bfloat16)
-    mixed = jnp.dot(old_probs, cache_values, preferred_element_type=jnp.float32) + jnp.dot(
-        new_probs, value_new, preferred_element_type=jnp.float32
-    )
-    mixed = (
-        mixed.astype(jnp.bfloat16)
-        .reshape(group, tree, head_dim)
-        .transpose(1, 0, 2)
-        .reshape(tree, group * head_dim)
-    )
-    return (mixed, jnp.concatenate([key_new, value_new], axis=-1))
-
-
 def place():
     r = lax.axis_index("req")
     return r // (NY * NC), (r // NC) % NY, r % NC, lax.axis_index("head")
@@ -111,108 +44,216 @@
     )
 
 
-def gather_kernel(rows_ref, table_ref, rows_out, table_out, send, recv, local):
+def attend_kernel(
+    rows_ref, gain1_ref, gain2_ref, cols_ref, accepted_ref, freq_ref, table_ref, cache_hbm, qkv_hbm,
+    out_hbm, resid_out, normed_out, table_out, kv_out,
+    mine, every, cache, qkv, out_w, terms, total, got, mine2, reach_v, cos_v, sin_v,
+    load, send, recv, send_t, recv_t, send2, recv2, send3, recv3,
+):
     z, y, c, x = place()
-    peers = [device(z, y, c, (x + d) % NX) for d in (1, 3, 2)]
-    rendezvous(peers)
-    copies = []
-    for i, peer in enumerate(peers):
-        copies.append(remote(table_ref, table_out.at[x], send.at[1, i], recv.at[1, i], peer))
-        copies.append(remote(rows_ref, rows_out.at[x], send.at[0, i], recv.at[0, i], peer))
-    for copy in copies:
-        copy.start()
-    own = [
-        pltpu.make_async_copy(rows_ref, rows_out.at[x], local.at[0]),
-        pltpu.make_async_copy(table_ref, table_out.at[x], local.at[1]),
+    tree, width = rows_ref.shape
+    peers = [(x + d) % NX for d in (1, 3, 2)]
+    loads = [pltpu.make_async_copy(qkv_hbm, qkv, load.at[0])]
+    for d in (0, 1, 3, 2):
+        p = (x + d) % NX
+        loads.append(pltpu.make_async_copy(cache_hbm.at[p], cache.at[p], load.at[2 + d]))
+    loads.append(pltpu.make_async_copy(out_hbm, out_w, load.at[1]))
+    for copy in loads:
+        copy.start()
+    own = rms_norm(rows_ref[...], gain1_ref[...])
+    mine[...] = own
+    rendezvous([device(z, y, c, p) for p in peers])
+    outgoing = []
+    for d in (1, 3, 2):
+        peer = device(z, y, c, (x + d) % NX)
+        outgoing.append(
+            remote(mine, every.at[x], send.at[d - 1], recv.at[d - 1], peer)
+        )
+        outgoing.append(
+            remote(table_ref, table_out.at[x], send_t.at[d - 1], recv_t.at[d - 1], peer)
+        )
+    for copy in outgoing[0::2] + outgoing[1::2]:
+        copy.start()
+    every[x] = own
+    table_out[x] = table_ref[...]
+
+    count = NX * tree
+    row = lax.broadcasted_iota(jnp.int32, (count, count), 0)
+    column = lax.broadcasted_iota(jnp.int32, (count, count), 1)
+    parent = cols_ref[:, 0:1]
+    base = row - row % tree
+    linked = ((parent >= 0) & (base + parent == column)) | (row == column)
+    reach = jnp.where(linked, 1.0, 0.0)
+    for turn in range((tree - 1).bit_length()):
+        near = reach.astype(jnp.bfloat16)
+        reach = jnp.minimum(jnp.dot(near, near, preferred_element_type=jnp.float32), 1.0)
+    depth = jnp.sum(reach, axis=-1, keepdims=True) - 1.0
+    for r in range(NX):
+        reach_v[r] = reach[r * tree : (r + 1) * tree, r * tree : (r + 1) * tree]
+    position = cols_ref[:, 1:2].astype(jnp.float32) + depth
+    angle = position * freq_ref[...]
+    head_dim = freq_ref.shape[1]
+    lane = lax.broadcasted_iota(jnp.int32, (count, head_dim), 1)
+    cos_v[...] = jnp.cos(angle)
+    sine = jnp.sin(angle)
+    sin_v[...] = jnp.where(lane < head_dim // 2, -sine, sine)
+    loads[0].wait()
+    group = qkv.shape[1] // head_dim - 2
+    scale = 1.0 / math.sqrt(head_dim)
+
+    def step(s, carry):
+        d = s + s // 2 - 2 * (s // 3)
+        p = (x + d) % NX
+
+        @pl.when(s > 0)
+        def _():
+            remote(
+                mine, every.at[p], send.at[3 - d], recv.at[3 - d], device(z, y, c, p)
+            ).wait_recv()
+
+        part = pl.ds(pl.multiple_of(p * tree, tree), tree)
+        projected = jnp.dot(every[p], qkv[...], preferred_element_type=jnp.float32)
+        cosine, sine = cos_v[part], sin_v[part]
+
+        def turned(v):
+            return (v * cosine + pltpu.roll(v, head_dim // 2, 1) * sine).astype(jnp.bfloat16)
+
+        query = jnp.concatenate(
+            [turned(projected[:, h * head_dim : (h + 1) * head_dim]) for h in range(group)], axis=0
+        )
+        key_new = turned(projected[:, group * head_dim : (group + 1) * head_dim])
+        value_new = projected[:, (group + 1) * head_dim :].astype(jnp.bfloat16)
+        fresh = jnp.concatenate([key_new, value_new], axis=1)
+        chosen = accepted_ref[p] == lax.broadcasted_iota(
+            jnp.int32, (accepted_ref.shape[1], tree), 1
+        )
+        kv_out[p, 0] = jnp.dot(
+            jnp.where(chosen, 1.0, 0.0).astype(jnp.bfloat16), fresh,
+            preferred_element_type=jnp.float32,
+        ).astype(jnp.bfloat16)
+
+        pltpu.make_async_copy(cache_hbm.at[p], cache.at[p], load.at[2 + d]).wait()
+        nt = (((1,), (1,)), ((), ()))
+        slots = cache.shape[1]
+        length = cols_ref[pl.ds(pl.multiple_of(p * tree, tree), 1), 1:2]
+        visible = lax.broadcasted_iota(jnp.int32, (1, slots), 1) < length
+        old = lax.dot_general(
+            query, cache[p, :, :head_dim], nt, preferred_element_type=jnp.float32
+        ) * scale
+        new = lax.dot_general(query, key_new, nt, preferred_element_type=jnp.float32) * scale
+        old = jnp.where(visible, old, -1e30)
+        seen = jnp.concatenate([reach_v[p]] * group, axis=0)
+        new = jnp.where(seen > 0.5, new, -1e30)
+        peak = jnp.maximum(
+            jnp.max(old, axis=-1, keepdims=True), jnp.max(new, axis=-1, keepdims=True)
+        )
+        old = jnp.exp(old - peak)
+        new = jnp.exp(new - peak)
+        inverse = 1.0 / (
+            jnp.sum(old, axis=-1, keepdims=True) + jnp.sum(new, axis=-1, keepdims=True)
+        )
+        mixed = jnp.dot(
+            (old * inverse).astype(jnp.bfloat16), cache[p, :, head_dim:],
+            preferred_element_type=jnp.float32,
+        ) + jnp.dot(
+            (new * inverse).astype(jnp.bfloat16), value_new, preferred_element_type=jnp.float32
+        )
+        mixed = mixed.astype(jnp.bfloat16)
+        mixed = jnp.concatenate([mixed[h * tree : (h + 1) * tree] for h in range(group)], axis=1)
+
+        @pl.when(s == 0)
+        def _():
+            loads[-1].wait()
+
+        term = jnp.dot(mixed, out_w[...], preferred_element_type=jnp.float32)
+
+        @pl.when(s == 0)
+        def _():
+            total[...] = term + rows_ref[...].astype(jnp.float32)
+
+        @pl.when(s > 0)
+        def _():
+            terms[d - 1] = term.astype(jnp.bfloat16)
+            remote(
+                terms.at[d - 1], got.at[d - 1], send2.at[d - 1], recv2.at[d - 1],
+                device(z, y, c, p),
+            ).start()
+
+        return carry
+
+    lax.fori_loop(0, NX, step, 0)
+    returns = [
+        remote(
+            terms.at[d - 1], got.at[d - 1], send2.at[d - 1], recv2.at[d - 1],
+            device(z, y, c, (x + d) % NX),
+        )
+        for d in (1, 3, 2)
     ]
-    for copy in own:
-        copy.start()
-    for copy in own + copies:
+    for copy in returns:
+        copy.wait_recv()
+    resid = total[...]
+    for i in range(3):
+        resid = resid + got[i].astype(jnp.float32)
+    resid = resid.astype(jnp.bfloat16)
+    resid_out[...] = resid
+    normed = rms_norm(resid, gain2_ref[...])
+    mine2[...] = normed
+    last = [
+        remote(mine2, normed_out.at[x], send3.at[d - 1], recv3.at[d - 1], device(z, y, c, (x + d) % NX))
+        for d in (1, 3, 2)
+    ]
+    for copy in last:
+        copy.start()
+    normed_out[x] = normed
+    for copy in returns + outgoing[0::2]:
+        copy.wait_send()
+    for copy in outgoing[1::2] + last:
         copy.wait()
 
 
-def gather_rows(rows, table):
+def attend(rows, gain1, gain2, parents, lengths, accepted, table, cache, w_qkv, w_out):
+    tree, width = rows.shape
+    slots, pair = cache.shape[-2:]
+    head_dim = pair // 2
+    half = head_dim // 2
+    frequency = ROPE_BASE ** (-jnp.arange(half, dtype=jnp.float32) / half)
+    frequency = jnp.concatenate([frequency, frequency])[None]
+    lengths = jnp.broadcast_to(lengths[:, None], parents.shape)
+    cols = jnp.stack([parents.reshape(-1), lengths.reshape(-1)], axis=1)
+    bf16 = jnp.bfloat16
+    sem = pltpu.SemaphoreType.DMA((3,))
+    hbm = pl.BlockSpec(memory_space=pl.ANY)
     return pl.pallas_call(
-        gather_kernel,
+        attend_kernel,
         out_shape=(
-            jax.ShapeDtypeStruct((NX,) + rows.shape, rows.dtype),
+            jax.ShapeDtypeStruct((tree, width), bf16),
+            jax.ShapeDtypeStruct((NX, tree, width), bf16),
             jax.ShapeDtypeStruct((NX,) + table.shape, table.dtype),
+            jax.ShapeDtypeStruct((NX, 1, accepted.shape[1], pair), bf16),
         ),
-        in_specs=[VMEM, VMEM],
-        out_specs=(VMEM, VMEM),
+        in_specs=[VMEM] * 7 + [hbm] * 3,
+        out_specs=(VMEM,) * 4,
         scratch_shapes=[
-            pltpu.SemaphoreType.DMA((2, 3)),
-            pltpu.SemaphoreType.DMA((2, 3)),
-            pltpu.SemaphoreType.DMA((2,)),
-        ],
+            pltpu.VMEM((tree, width), bf16),
+            pltpu.VMEM((NX, tree, width), bf16),
+            pltpu.VMEM((NX, slots, pair), bf16),
+            pltpu.VMEM(w_qkv.shape, bf16),
+            pltpu.VMEM(w_out.shape, bf16),
+            pltpu.VMEM((3, tree, width), bf16),
+            pltpu.VMEM((tree, width), jnp.float32),
+            pltpu.VMEM((3, tree, width), bf16),
+            pltpu.VMEM((tree, width), bf16),
+            pltpu.VMEM((NX, tree, tree), jnp.float32),
+            pltpu.VMEM((NX * tree, head_dim), jnp.float32),
+            pltpu.VMEM((NX * tree, head_dim), jnp.float32),
+            pltpu.SemaphoreType.DMA((6,)),
+        ] + [sem] * 8,
         compiler_params=pltpu.CompilerParams(collective_id=1, has_side_effects=True),
-        name="gather_rows",
-    )(rows, table)
-
-
-PIECES = 2
-
-
-def resid_kernel(term_ref, own_ref, gain_ref, resid_out, normed_out, got, mine, send, recv, send2, recv2):
-    z, y, c, x = place()
-    peers = [(x + d) % NX for d in (1, 3, 2)]
-    rendezvous([device(z, y, c, p) for p in peers])
-    rows = own_ref.shape[0] // PIECES
-    first = []
-    for piece in range(PIECES):
-        part = pl.ds(piece * rows, rows)
-        for i, p in enumerate(peers):
-            copy = remote(
-                term_ref.at[p, part], got.at[i, part], send.at[piece, i], recv.at[piece, i],
-                device(z, y, c, p),
-            )
-            copy.start()
-            first.append(copy)
-    second = []
-    for piece in range(PIECES):
-        part = pl.ds(piece * rows, rows)
-        for i in range(3):
-            first[piece * 3 + i].wait_recv()
-        total = own_ref[part]
-        for i in range(3):
-            total = total + got[i, part].astype(jnp.float32)
-        resid = total.astype(jnp.bfloat16)
-        resid_out[part] = resid
-        normed = rms_norm(resid, gain_ref[...])
-        mine[part] = normed
-        normed_out[x, part] = normed
-        for i, p in enumerate(peers):
-            copy = remote(
-                mine.at[part], normed_out.at[x, part], send2.at[piece, i], recv2.at[piece, i],
-                device(z, y, c, p),
-            )
-            copy.start()
-            second.append(copy)
-    for copy in first:
-        copy.wait_send()
-    for copy in second:
-        copy.wait()
-
-
-def resid_rows(term, own, gain):
-    rows, width = own.shape
-    sem = pltpu.SemaphoreType.DMA((PIECES, 3))
-    return pl.pallas_call(
-        resid_kernel,
-        out_shape=(
-            jax.ShapeDtypeStruct((rows, width), jnp.bfloat16),
-            jax.ShapeDtypeStruct((NX, rows, width), jnp.bfloat16),
-        ),
-        in_specs=[VMEM] * 3,
-        out_specs=(VMEM, VMEM),
-        scratch_shapes=[
-            pltpu.VMEM((3, rows, width), jnp.bfloat16),
-            pltpu.VMEM((rows, width), jnp.bfloat16),
-            sem, sem, sem, sem,
-        ],
-        compiler_params=pltpu.CompilerParams(collective_id=2, has_side_effects=True),
-        name="resid_rows",
-    )(term, own, gain)
+        name="attend",
+    )(
+        rows, gain1[None], gain2[None], cols, accepted[:, :, None], frequency, table,
+        cache.reshape(NX, slots, pair), w_qkv, w_out,
+    )
 
 
 def exchange_kernel(src, out, mid_y, mid_z, send1, recv1, send2, recv2, local):
@@ -359,32 +400,14 @@
     tree, width = tokens.shape[1:]
     own_rows = tokens[0]
     x = lax.axis_index("head")
-    local_heads = cache.shape[1]
-    head_dim = cache.shape[3] // 2
-    group = w_qkv.shape[1] // (local_heads * head_dim) - 2
     top_count = routes.shape[2]
     expert_count = router.shape[1]
     capacity = 4 * tree * top_count // (3 * expert_count)
 
     table = jnp.pad(routes[0].T, ((0, 8 - top_count), (0, 128 - tree)))
-    normed_all, table_all = gather_rows(rms_norm(own_rows, attn_gain), table)
-
-    projected = jnp.dot(
-        normed_all.reshape(NX * tree, width), w_qkv, preferred_element_type=jnp.float32
-    )
-    projected = projected.reshape(NX, tree, local_heads, group + 2, head_dim).transpose(
-        0, 2, 3, 1, 4
-    )
-    reach, depth = ancestry(parents)
-    positions = lengths[:, None].astype(jnp.float32) + depth
-    inner_map = jax.vmap(head_group, in_axes=(0, None, None, None, 0))
-    mixed, fresh = jax.vmap(inner_map)(projected, positions, lengths, reach, cache)
-    mixed = mixed.transpose(0, 2, 1, 3).reshape(NX * tree, local_heads * group * head_dim)
-    accepted_kv = jnp.take_along_axis(fresh, accepted[:, None, :, None], axis=2)
-
-    term = jnp.dot(mixed, w_out, preferred_element_type=jnp.float32).reshape(NX, tree, width)
-    own_term = lax.dynamic_index_in_dim(term, x, 0, keepdims=False) + own_rows.astype(jnp.float32)
-    resid, normed2 = resid_rows(term.astype(jnp.bfloat16), own_term, ffn_gain[None])
+    resid, normed2, table_all, accepted_kv = attend(
+        own_rows, attn_gain, ffn_gain, parents, lengths, accepted, table, cache, w_qkv, w_out
+    )
     normed2 = normed2.reshape(NX * tree, width)
 
     choose = table_all[:, :top_count, :tree]

time: 284 us -> 243 us (0.86)
  matrix products: 57.8 us -> 39.6 us
  other arithmetic: 22.3 us -> 11.4 us
  local copies, waits for them, and re-layouts: 24.1 us -> 15.2 us
  Pallas kernels: 178 us -> 175 us
    dot_general x9 -> x0, matrix products: 18.5 us -> none  [the longest x1 4.13 us: body(): jnp.dot(normed_all.reshape(NX * tree, width), w_qkv, preferred_element_ty...]
    unnamed x37 -> x19, local copies, waits for them, and re-layouts: 7.36 us -> 3 us
    gt x2 -> x0, local copies, waits for them, and re-layouts: 3.27 us -> none  [head_group(): jnp.tile(reach, (group, 1)) > 0.5]
    reduce_sum x3 -> x0, other arithmetic: 3.23 us -> none  [the longest x1 1.92 us: head_group(): jnp.sum(old_weights, axis=-1, keepdims=True)]
    pallas_call x2 -> x1, Pallas kernels: 45.3 us -> 43 us  [attend(): pl.pallas_call(attend_kernel, out_shape=(jax.ShapeDtypeStruct((tree, widt...]
where the time goes in v2:
time: 243 us; the launch traced here: 242 us
  Pallas kernels  175 us (72%)
  matrix products  39.6 us (16%)
  local copies, waits for them, and re-layouts  15.2 us (6%)
  other arithmetic  11.4 us (5%)
    pallas_call x2, Pallas kernels, exchange(): pl.pallas_call(exchange_kernel, out_shape=jax.ShapeDtypeStruct(blocks.sha...  115 us
    pallas_call x1, Pallas kernels, attend(): pl.pallas_call(attend_kernel, out_shape=(jax.ShapeDtypeStruct((tree, widt...  43 us
    pallas_call x1, Pallas kernels, final_rows(): pl.pallas_call(final_kernel, out_shape=jax.ShapeDtypeStruct((rows, width)...  17.3 us
    dot_general x1, matrix products, expert_half(): both = jnp.dot(rows, inner, preferred_element_type=jnp.float32)  10.4 us
    dot_general x1, matrix products, body(): jnp.dot(hidden, shared_down, preferred_element_type=jnp.float32)  6.83 us
    dot_general x1, matrix products, expert_half(): jnp.dot(hidden, outer, preferred_element_type=jnp.float32)  5.4 us
    dot_general x1, matrix products, body(): jnp.dot(weight_low, returned, preferred_element_type=jnp.float32)  4.95 us
    dot_general x1, matrix products, body(): jnp.dot(weight_high, returned, preferred_element_type=jnp.float32)  4.94 us

profile of v2, /device:TPU:1, one launch (start us, length us, event | category | flops | bytes accessed | tf_op | source)
XLA Modules:
  0.0 242.2 jit_solution(11431825394664564482)
XLA Ops:
  0.7 0.9 broadcast_in_dim.50
  1.6 0.8 stack_reshape.6
  2.4 0.8 copy.39.cols_ref
  3.2 1.4 copy.40.accepted_ref
  4.6 0.7 copy.56
  5.3 0.6 pad.4.table_ref
  5.9 0.6 maximum_bitcast_fusion.freq_ref
  6.5 43.0 %attend.1 = (bf16[64,2048]{1,0:T(8,128)(2,1)}, bf16[4,64,2048]{2,1,0:T(8,128)(2,1)}, s32[4,8,128]{2,1,0:T(8,128)}, bf16[4,1,8,256]{3,2,1,0:T(8,128)(2,1)}) custom-call(bf16[64,2048]{1,0:T(8,128)(2,1)} %bitcast.79, f32[1,2048]{1,0:T(1,128)} %bitcast.84, f32[1,2048]{1,0:T(1,128)} %bitcast.85, s32[256,2]{1,0:T(8,128)} %copy.39.cols_ref, ...), custom_call_target="tpu_custom_call" | custom-call | tf_op jit(solution)/shard_map/attend/pallas_call | solution.py:226
  49.5 1.0 fusion.13
  50.7 1.7 select_reduce_fusion
  53.2 0.7 fusion.20
  54.1 0.7 broadcast_and_fusion
  54.8 1.6 and.47
  56.4 4.5 %convolution_convert_fusion.1 = bf16[1024,2048]{1,0:T(8,128)(2,1)} fusion(pred[256,1024]{0,1:T(32,128)(4,1)} %and.47, bf16[256,2048]{1,0:T(8,128)(2,1)} %bitcast.69), kind=kOutput, calls=%fused_computation.3 | convolution fusion | flops 1075838976 | bytes 5505024 | tf_op jit(solution)/shard_map/dot_general | solution.py:442
  60.9 60.2 %exchange.2 = bf16[4,4,2,32,2048]{4,3,2,1,0:T(8,128)(2,1)} custom-call(bf16[4,4,2,32,2048]{4,3,2,1,0:T(8,128)(2,1)} %bitcast.65), custom_call_target="tpu_custom_call" | custom-call | tf_op jit(solution)/shard_map/exchange/pallas_call | solution.py:320
  121.1 10.4 %fusion = f32[1024,1408]{1,0:T(8,128)S(1)} fusion(bf16[1024,2048]{1,0:T(8,128)(2,1)} %bitcast.75, bf16[1,2048,1408]{2,1,0:T(8,128)(2,1)} %param.32), kind=kOutput, calls=%fused_computation | convolution fusion | flops 5905580032 | bytes 15728640 | tf_op jit(solution)/shard_map/dot_general | solution.py:375
  131.6 5.4 %convolution_convert_fusion = bf16[1024,2048]{1,0:T(8,128)(2,1)} fusion(bf16[1,704,2048]{2,1,0:T(8,128)(2,1)S(1)} %copy-done, f32[1024,1408]{1,0:T(8,128)S(1)} %fusion), kind=kOutput, calls=%fused_computation.2 | convolution fusion | flops 2959212544 | bytes 13369344 | tf_op jit(solution)/shard_map/dot_general | solution.py:378
  137.0 54.5 %exchange.3 = bf16[4,4,2,32,2048]{4,3,2,1,0:T(8,128)(2,1)} custom-call(bf16[4,4,2,32,2048]{4,3,2,1,0:T(8,128)(2,1)} %bitcast.76), custom_call_target="tpu_custom_call" | custom-call | tf_op jit(solution)/shard_map/exchange/pallas_call | solution.py:320
  191.5 1.7 select_convert_fusion
  193.3 2.7 %convert_element_type.70 = bf16[256,1024]{0,1:T(8,128)(2,1)} reshape(bf16[4,64,32,4,8]{1,0,4,3,2:T(4,128)(2,1)} %select_convert_fusion) | data formatting | bytes 1048576 | tf_op jit(solution)/shard_map/convert_element_type | solution.py:440
  196.0 4.9 %fusion.34 = f32[256,2048]{1,0:T(8,128)} fusion(bf16[256,1024]{0,1:T(8,128)(2,1)} %convert_element_type.70, bf16[1024,2048]{1,0:T(8,128)(2,1)} %bitcast.73), kind=kOutput, calls=%fused_computation.58 | convolution fusion | flops 1073741824 | bytes 6815744 | tf_op jit(solution)/shard_map/dot_general | solution.py:457
  200.9 1.8 fusion.5
  202.8 2.1 convert_element_type.76
  204.9 5.0 %fusion.35 = f32[256,2048]{1,0:T(8,128)} fusion(bf16[256,1024]{0,1:T(8,128)(2,1)S(1)} %convert_element_type.76, bf16[1024,2048]{1,0:T(8,128)(2,1)} %bitcast.74), kind=kOutput, calls=%fused_computation.59 | convolution fusion | flops 1073741824 | bytes 6815744 | tf_op jit(solution)/shard_map/dot_general | solution.py:458
  209.9 0.6 fusion.33
  210.4 6.8 %fusion.4 = f32[256,2048]{1,0:T(8,128)} fusion(f32[256,2048]{1,0:T(8,128)} %fusion.35, f32[256,2048]{1,0:T(8,128)} %fusion.34, bf16[352,2048]{1,0:T(8,128)(2,1)} %param.30, bf16[256,2048]{1,0:T(8,128)(2,1)} %bitcast.70, bf16[2048,352]{0,1:T(8,128)(2,1)} %param.29, f32[256,352]{0,1:T(8,128)S(1)} %fusion.33), kind=kOutput, calls=%fused_computation.8 | convolution fusion | flops 739786752 | bytes 10584064 | tf_op jit(solution)/shard_map/dot_general | solution.py:456
  217.3 1.9 bitcast_add_fusion.own_ref
  219.2 2.7 %convert_element_type.77.part_ref = bf16[4,64,2048]{2,1,0:T(8,128)(2,1)} convert(f32[4,64,2048]{2,1,0:T(8,128)} %bitcast.67) | non-fusion elementwise | flops 524288 | bytes 3145728 | tf_op jit(solution)/shard_map/convert_element_type | solution.py:461
  221.9 0.7 copy.46.live_ref
  222.6 17.3 %final_rows.1 = bf16[64,2048]{1,0:T(8,128)(2,1)} custom-call(bf16[4,64,2048]{2,1,0:T(8,128)(2,1)} %convert_element_type.77.part_ref, f32[64,2048]{1,0:T(8,128)} %bitcast_add_fusion.own_ref, s32[64,1]{1,0:T(8,128)} %copy.46.live_ref), custom_call_target="tpu_custom_call" | custom-call | tf_op jit(solution)/shard_map/final_rows/pallas_call | solution.py:359
  239.9 1.7 copy.61
  241.6 0.6 copy.62
  (30 shorter events, 1.2 us)
Async XLA Ops:
  0.6 130.9 %copy-start = (bf16[1,704,2048]{2,1,0:T(8,128)(2,1)S(1)}, bf16[1,704,2048]{2,1,0:T(8,128)(2,1)}, u32[]{:S(2)}) copy-start(bf16[1,704,2048]{2,1,0:T(8,128)(2,1)} %param.33) | copy-start | bytes 8650756
  6.5 44.2 %copy-start.7 = (bf16[2048,64]{0,1:T(8,128)(2,1)S(1)}, bf16[2048,64]{0,1:T(8,128)(2,1)}, u32[]{:S(2)}) copy-start(bf16[2048,64]{0,1:T(8,128)(2,1)} %param.31) | copy-start | bytes 786436
  137.0 54.6 %copy-start.3 = (f32[4,64,32]{1,0,2:T(4,128)S(1)}, f32[4,64,32]{1,0,2:T(4,128)}, u32[]{:S(2)}) copy-start(f32[4,64,32]{1,0,2:T(4,128)} %get-tuple-element.14) | copy-start | bytes 98308
  204.9 5.0 %copy-start.1 = (bf16[4,64,2048]{2,1,0:T(8,128)(2,1)S(1)}, bf16[4,64,2048]{2,1,0:T(8,128)(2,1)}, u32[]{:S(2)}) copy-start(bf16[4,64,2048]{2,1,0:T(8,128)(2,1)} %get-tuple-element.6) | copy-start | bytes 3145732
  204.9 5.0 %copy-start.2 = (bf16[2048,352]{0,1:T(8,128)(2,1)S(1)}, bf16[2048,352]{0,1:T(8,128)(2,1)}, u32[]{:S(2)}) copy-start(bf16[2048,352]{0,1:T(8,128)(2,1)} %param.28) | copy-start | bytes 4325380
  210.4 6.8 %copy-start.4 = (bf16[64,2048]{1,0:T(8,128)(2,1)S(1)}, bf16[64,2048]{1,0:T(8,128)(2,1)}, u32[]{:S(2)}) copy-start(bf16[64,2048]{1,0:T(8,128)(2,1)} %get-tuple-element.8) | copy-start | bytes 786436
  217.3 4.6 %copy-start.6 = (s32[1,64]{1,0:T(1,128)S(1)}, s32[1,64]{1,0:T(1,128)}, u32[]{:S(2)}) copy-start(s32[1,64]{1,0:T(1,128)} %param.18) | copy-start | bytes 772
  219.2 22.4 %copy-start.5 = (bf16[4,1,8,256]{3,2,1,0:T(8,128)(2,1)S(1)}, bf16[4,1,8,256]{3,2,1,0:T(8,128)(2,1)}, u32[]{:S(2)}) copy-start(bf16[4,1,8,256]{3,2,1,0:T(8,128)(2,1)} %get-tuple-element.19) | copy-start | bytes 49156
